TPU v7x, 32 devices: a whole 2x2x4 slice. The times are simulated.
32 devices in a mesh: dp: 4 (over y, core), proto: 8 (over z, x).
Axes of the slice: x: 2, y: 2, z: 4, core: 2. Of those that a mesh axis runs over, the one named last changes fastest.
Arguments:
- student_rows: bfloat16 [64, 256, 256], P('dp'), may hold values from -0.375 to 0.375
- teacher_rows: bfloat16 [64, 256, 256], P('dp'), may hold values from -0.375 to 0.375
- student_proto: bfloat16 [256, 131072], P(None, 'proto'), may hold values from -0.375 to 0.375
- teacher_proto: bfloat16 [256, 131072], P(None, 'proto'), may hold values from -0.375 to 0.375
- center: float32 [131072], P('proto'), may hold values from -0.05 to 0.05
- counts: int32 [64], replicated, may hold values from 1 to 128, 6144 in all
- mask_order: int32 [64, 256], P('dp'), may hold values from 0 to 255, each once within a row
Outputs:
- row_loss: float32 [4, 1536], P('dp')
- student_grad: bfloat16 [4, 1536, 256], P('dp')
Inputs may be any that keep to these rules, and one draw needn't show every extreme that they name: counts sum to 6144, and some image has exactly 128. `mask_order`: each row is a permutation of the patch positions; image i's masked patches are its first counts[i] entries.
All inputs are finite; a program needn't handle non-finite values.
Results may differ from a plain program's by a relative error of at most 0.002.
The roundings to bfloat16 on the way count: a program that leaves them out, or rounds other values in their place, can miss the bound.
Values may be sent and summed in bfloat16 or wider, within the bound.
No kernel may reach another device: no remote copies, remote signals or barrier semaphores. Data moves between devices by JAX's collectives and lax.ppermute only.
A program may use at most 320 MiB of HBM per device.

v0:
```python
import jax
import jax.numpy as jnp
from jax import lax
from jax.sharding import PartitionSpec as P

MASK_IMG = 96
STUDENT_TEMP = 0.1
TEACHER_TEMP = 0.07
EPSILON = 1e-06


def norm_columns(weights):
    wide = weights.astype(jnp.float32)
    return (wide / jnp.sqrt(jnp.sum(wide * wide, axis=0, keepdims=True) + EPSILON)).astype(
        jnp.bfloat16
    )


def backward(student_in, student_norm, feature_grad):
    inner = jnp.sum(student_in * feature_grad, axis=-1, keepdims=True)
    return feature_grad / student_norm - student_in * inner / (
        student_norm * student_norm * student_norm
    )


def proto_head(student_part, teacher_part, student_cols, teacher_cols, center):
    student_in = student_part.astype(jnp.float32)
    teacher_in = teacher_part.astype(jnp.float32)
    student_norm = jnp.sqrt(jnp.sum(student_in * student_in, axis=-1, keepdims=True) + EPSILON)
    teacher_norm = jnp.sqrt(jnp.sum(teacher_in * teacher_in, axis=-1, keepdims=True) + EPSILON)
    student_unit = (student_in / student_norm).astype(jnp.bfloat16)
    teacher_unit = (teacher_in / teacher_norm).astype(jnp.bfloat16)
    student_logit = jnp.dot(student_unit, student_cols, preferred_element_type=jnp.float32)
    teacher_logit = jnp.dot(teacher_unit, teacher_cols, preferred_element_type=jnp.float32)
    student_exp = jnp.exp(student_logit / STUDENT_TEMP)
    teacher_exp = jnp.exp((teacher_logit - center[None, :]) / TEACHER_TEMP)
    totals = lax.psum(
        (
            jnp.sum(student_exp, axis=1),
            jnp.sum(teacher_exp, axis=1),
            jnp.sum(teacher_exp * (student_logit / STUDENT_TEMP), axis=1),
        ),
        "proto",
    )
    student_sum, teacher_sum, cross_sum = totals
    row_losses = jnp.log(student_sum) - cross_sum / teacher_sum
    logit_grad = (
        (student_exp / student_sum[:, None] - teacher_exp / teacher_sum[:, None]) / STUDENT_TEMP
    ).astype(jnp.bfloat16)
    feature_grad = lax.dot_general(
        logit_grad, student_cols, (((1,), (1,)), ((), ())), preferred_element_type=jnp.float32
    )
    feature_grad = lax.psum(feature_grad, "proto")
    input_grad = backward(student_in, student_norm, feature_grad)
    return (row_losses, input_grad)


def local(student_rows, teacher_rows, student_proto, teacher_proto, center, counts, mask_order):
    img_dev, patches, feature_width = student_rows.shape
    dp_count = lax.axis_size("dp")
    dp_index = lax.axis_index("dp")
    capacity = img_dev * (patches // 2)
    slot_count = (capacity + dp_count - 1) // dp_count
    mask_dev = MASK_IMG * img_dev
    dev_counts = jnp.sum(counts.reshape(dp_count, img_dev), axis=1)
    dev_ends = jnp.cumsum(dev_counts)
    dev_starts = dev_ends - dev_counts
    is_owner = jnp.arange(dp_count, dtype=jnp.int32) == dp_index
    own_start = jnp.sum(jnp.where(is_owner, dev_starts, 0))
    own_count = jnp.sum(jnp.where(is_owner, dev_counts, 0))
    local_counts = lax.dynamic_slice_in_dim(counts, dp_index * img_dev, img_dev)
    local_ends = jnp.cumsum(local_counts)
    local_starts = local_ends - local_counts
    order_flat = mask_order.reshape(-1)
    targets = jnp.arange(dp_count, dtype=jnp.int32)[:, None]
    slot_ids = jnp.arange(slot_count, dtype=jnp.int32)[None, :]
    send_pos = jnp.mod(targets - own_start, dp_count) + slot_ids * dp_count
    send_valid = send_pos < own_count
    balanced = jnp.arange(mask_dev, dtype=jnp.int32)
    global_pos = balanced * dp_count + dp_index
    source = jnp.sum((global_pos[:, None] >= dev_ends[None, :]).astype(jnp.int32), axis=1)
    source_start = jnp.take(dev_starts, source)
    first_pos = source_start + jnp.mod(dp_index - source_start, dp_count)
    receive_ids = source * slot_count + (global_pos - first_pos) // dp_count
    student_flat = student_rows.reshape(img_dev * patches, feature_width)
    teacher_flat = teacher_rows.reshape(img_dev * patches, feature_width)
    student_cols = norm_columns(student_proto)
    teacher_cols = norm_columns(teacher_proto)
    image_ids = jnp.minimum(
        jnp.sum((send_pos[..., None] >= local_ends).astype(jnp.int32), axis=-1), img_dev - 1
    )
    within = jnp.clip(send_pos - jnp.take(local_starts, image_ids), 0, patches - 1)
    patch_ids = jnp.take(order_flat, image_ids * patches + within)
    row_ids = image_ids * patches + patch_ids
    keep_mask = send_valid[..., None]
    send_student = jnp.where(keep_mask, jnp.take(student_flat, row_ids, axis=0), 0)
    send_teacher = jnp.where(keep_mask, jnp.take(teacher_flat, row_ids, axis=0), 0)
    got_student, got_teacher = (
        lax.all_to_all(send_student, "dp", split_axis=0, concat_axis=0, tiled=True),
        lax.all_to_all(send_teacher, "dp", split_axis=0, concat_axis=0, tiled=True),
    )
    student_part = jnp.take(
        got_student.reshape(dp_count * slot_count, feature_width), receive_ids, axis=0
    )
    teacher_part = jnp.take(
        got_teacher.reshape(dp_count * slot_count, feature_width), receive_ids, axis=0
    )
    row_losses, input_grad = proto_head(
        student_part, teacher_part, student_cols, teacher_cols, center
    )
    return (row_losses[None, :], input_grad.astype(jnp.bfloat16)[None])


def solution(mesh):
    placed = (
        P("dp", None, None),
        P("dp", None, None),
        P(None, "proto"),
        P(None, "proto"),
        P("proto"),
        P(),
        P("dp", None),
    )
    return jax.shard_map(
        local,
        mesh=mesh,
        in_specs=placed,
        out_specs=(P("dp", None), P("dp", None, None)),
        check_vma=False,
    )
```

profile of v0, /device:TPU:0, one launch (start us, length us, event | category | flops | bytes accessed | tf_op | source)
XLA Modules:
  0.0 418.9 jit_solution(7376634795189560316)
XLA Ops:
  7.2 0.0 copy-start
  7.2 0.0 copy-start.9
  7.2 0.9 reshape.344
  8.1 0.7 dynamic-slice_bitcast_fusion
  8.8 0.1 copy.11
  8.9 0.1 reduce.1
  9.1 0.7 dynamic-slice_subtract_fusion
  9.8 0.1 reduce_sum.119
  9.9 0.2 reduce-window.16
  10.1 0.6 fusion.32
  10.7 0.7 and_select_fusion
  11.4 0.1 broadcast_add_fusion
  11.5 0.1 convert_reduce_fusion
  11.6 12.6 %gather_fusion = s32[2048]{0:T(1024)S(1)} fusion(s32[16]{0:T(128)S(1)} %dynamic-slice_subtract_fusion, s32[2048]{0:T(1024)S(1)} %broadcast_clamp_fusion.2), kind=kCustom, calls=%fused_computation.4 | custom fusion | bytes 24576 | tf_op jit(solution)/shard_map/jit(_take)/gather | solution.py:92
  24.3 0.0 copy-done.9
  24.3 0.1 fusion.26
  24.4 11.8 %gather_fusion.1 = s32[2048]{0:T(1024)S(1)} fusion(s32[4096]{0:T(1024)S(1)} %bitcast.43, s32[2048]{0:T(1024)S(1)} %broadcast_clamp_fusion.1), kind=kCustom, calls=%fused_computation.5 | custom fusion | bytes 24576 | tf_op jit(solution)/shard_map/jit(_take)/gather | solution.py:93
  36.2 0.7 compare_and_fusion.1
  36.9 0.0 copy-done
  37.0 7.5 %gather_fusion.4 = bf16[2048,256]{1,0:T(8,128)(2,1)S(1)} fusion(bf16[4096,256]{1,0:T(8,128)(2,1)S(1)} %bitcast.42, s32[2048]{0:T(1024)S(1)} %broadcast_clamp_fusion), kind=kCustom, calls=%fused_computation.2.clone | custom fusion | bytes 2105344 | tf_op jit(solution)/shard_map/jit(_take)/gather | solution.py:97
  44.5 10.3 %gather_fusion.2 = bf16[2048,256]{1,0:T(8,128)(2,1)} fusion(bf16[4096,256]{1,0:T(8,128)(2,1)} %bitcast.45, s32[2048]{0:T(1024)S(1)} %broadcast_clamp_fusion), kind=kCustom, calls=%fused_computation.clone | custom fusion | bytes 2105344 | tf_op jit(solution)/shard_map/jit(_take)/gather | solution.py:96
  54.8 3.7 select_select_fusion
  58.5 4.3 %all-to-all-start = ((bf16[4,512,256]{2,1,0:T(8,128)(2,1)}), bf16[4,512,256]{2,1,0:T(8,128)(2,1)S(1)}, u32[]{:S(2)}, u32[]{:S(2)}) async-start(bf16[4,512,256]{2,1,0:T(8,128)(2,1)} %get-tuple-element.21), calls=%async_computation | async-start | bytes 2097152 | tf_op jit(solution)/shard_map/all_to_all | solution.py:99
  62.7 5.1 %fusion.3 = f32[16384]{0:T(1024)S(1)} fusion(bf16[256,16384]{1,0:T(8,128)(2,1)} %param.14), kind=kLoop, calls=%fused_computation.17 | loop fusion | flops 12566528 | bytes 8454144 | tf_op jit(solution)/shard_map/reduce_sum | solution.py:14
  67.8 0.6 fusion.39
  68.5 0.1 convert_reduce_fusion.1
  68.6 2.5 fusion.31
  71.1 0.0 copy-start.6
  71.2 5.1 %fusion.1 = f32[16384]{0:T(1024)S(1)} fusion(bf16[256,16384]{1,0:T(8,128)(2,1)} %param.13), kind=kLoop, calls=%fused_computation.15 | loop fusion | flops 12566528 | bytes 8454144 | tf_op jit(solution)/shard_map/reduce_sum | solution.py:14
  76.3 0.9 all-to-all-done
  77.2 4.3 %all-to-all-start.1 = ((bf16[4,512,256]{2,1,0:T(8,128)(2,1)}), bf16[4,512,256]{2,1,0:T(8,128)(2,1)}, u32[]{:S(2)}, u32[]{:S(2)}) async-start(bf16[4,512,256]{2,1,0:T(8,128)(2,1)} %get-tuple-element.20), calls=%async_computation.1 | async-start | bytes 2097152 | tf_op jit(solution)/shard_map/all_to_all | solution.py:100
  81.4 0.2 all-reduce.3.cloned.1.call-start
  81.7 0.0 copy-start.11
  81.7 5.4 %gather_fusion.3 = bf16[1536,256]{1,0:T(8,128)(2,1)} fusion(bf16[2048,256]{1,0:T(8,128)(2,1)S(1)} %bitcast.44, s32[2048]{0:T(1024)S(1)} %pad_clamp_fusion), kind=kCustom, calls=%fused_computation.1.clone | custom fusion | bytes 1579008 | tf_op jit(solution)/shard_map/jit(_take)/gather | solution.py:102
  87.1 0.0 copy-start.1
  87.1 8.8 %all-to-all-done.1 = bf16[4,512,256]{2,1,0:T(8,128)(2,1)} async-done(((bf16[4,512,256]{2,1,0:T(8,128)(2,1)}), bf16[4,512,256]{2,1,0:T(8,128)(2,1)}, u32[]{:S(2)}, u32[]{:S(2)}) %all-to-all-start.1) | async-done | bytes 1048608 | tf_op jit(solution)/shard_map/all_to_all | solution.py:100
  95.9 5.9 %gather_fusion.5 = bf16[1536,256]{1,0:T(8,128)(2,1)} fusion(bf16[2048,256]{1,0:T(8,128)(2,1)} %bitcast.13, s32[2048]{0:T(1024)S(1)} %pad_clamp_fusion), kind=kCustom, calls=%fused_computation.3.clone | custom fusion | bytes 1579008 | tf_op jit(solution)/shard_map/jit(_take)/gather | solution.py:105
  101.8 2.2 fusion.9
  103.9 0.6 multiply_multiply_fusion
  104.6 0.0 copy-start.4
  104.6 0.0 copy-done.1
  104.6 1.8 fusion.16.clone.5
  106.3 0.0 copy-done.4
  106.3 0.0 copy-done.6
  106.4 0.0 copy-done.11
  106.4 0.0 copy-start.3
  106.4 39.1 %multiply_exponential_fusion = f32[1536,16384]{1,0:T(8,128)} fusion(f32[16384]{0:T(1024)S(1)} %copy-done.11, bf16[256,16384]{1,0:T(8,128)(2,1)} %param.14, f32[16384]{0:T(1024)S(1)} %add_sqrt_fusion, f32[1536]{0:T(1024)S(1)} %get-tuple-element.29, bf16[1536,256]{1,0:T(8,128)(2,1)} %gather_fusion.5, pred[1536]{0:T(1024)(128)(4,1)S(1)} %get-tuple-element.12), kind=kOutput, calls=%fused_computation.8 | convolution fusion | flops 12949389312 | bytes 109977088 | tf_op jit(solution)/shard_map/dot_general | solution.py:34
  145.4 0.0 copy-done.3
  145.4 70.0 %exponential_reduce_fusion = (f32[1536]{0:T(1024)S(1)}, f32[1536]{0:T(1024)S(1)}, f32[1536]{0:T(1024)S(1)}, f32[1536,16384]{1,0:T(8,128)}) fusion(f32[1536,16384]{1,0:T(8,128)} %multiply_exponential_fusion, bf16[256,16384]{1,0:T(8,128)(2,1)} %param.13, f32[16384]{0:T(1024)S(1)} %add_sqrt_fusion.1, bf16[1536,256]{1,0:T(8,128)(2,1)S(1)} %copy-done.3), kind=kOutput, calls=%fused_computation.9 | convolution fusion | flops 13023307776 | bytes 210585600 | tf_op jit(solution)/shard_map/dot_general | solution.py:33
  215.4 38.1 %all-reduce = (f32[1536]{0:T(1024)}, f32[1536]{0:T(1024)S(1)}, f32[1536]{0:T(1024)S(1)}) all-reduce(f32[1536]{0:T(1024)S(1)} %get-tuple-element.5, f32[1536]{0:T(1024)S(1)} %get-tuple-element.6, f32[1536]{0:T(1024)S(1)} %get-tuple-element.4), channel_id=1, replica_groups=mesh['dp'=4,'proto'=8] {'proto'}, use_global_device_ids=true, to_apply=%region_14.17 | all-reduce | flops 4608 | bytes 36864 | tf_op jit(solution)/shard_map/psum | solution.py:37
  253.5 0.0 copy-start.7
  253.5 0.0 copy-start.5
  253.6 0.0 copy-start.8
  253.6 67.1 %fusion = f32[1536,256]{1,0:T(8,128)} fusion(f32[1536,16384]{1,0:T(8,128)} %multiply_exponential_fusion, f32[1536,16384]{1,0:T(8,128)} %get-tuple-element.28, f32[1536]{0:T(1024)S(1)} %get-tuple-element.10, f32[1536]{0:T(1024)S(1)} %get-tuple-element.11, bf16[256,16384]{1,0:T(8,128)(2,1)} %param.13, f32[16384]{0:T(1024)S(1)} %add_sqrt_fusion.1), kind=kOutput, calls=%fused_computation.10 | convolution fusion | flops 13048479744 | bytes 211365888 | tf_op jit(solution)/shard_map/dot_general | solution.py:50
  320.7 0.0 all-reduce.3.cloned.1.call-update
  320.7 0.0 copy-done.10
  320.8 0.6 broadcast_in_dim.84
  321.4 84.9 %all-reduce.3.cloned.1.call-done = f32[1536,256]{1,0:T(8,128)} async-done(((f32[1536,256]{1,0:T(8,128)}), f32[1536,256]{1,0:T(8,128)}) %all-reduce.3.cloned.1.call-update) | async-done | bytes 1572880 | tf_op jit(solution)/shard_map/psum | solution.py:53
  406.3 0.0 copy-done.2
  406.3 0.0 copy-done.7
  406.3 1.9 fusion.11
  408.2 0.0 copy-done.5
  408.2 0.0 copy-done.8
  408.2 3.8 fusion.20
  (21 shorter events, 0.2 us)
Async XLA Ops:
  7.2 29.8 %copy-start = (bf16[16,256,256]{2,1,0:T(8,128)(2,1)S(1)}, bf16[16,256,256]{2,1,0:T(8,128)(2,1)}, u32[]{:S(2)}) copy-start(bf16[16,256,256]{2,1,0:T(8,128)(2,1)} %param.12) | copy-start | bytes 6291460
  7.2 17.1 %copy-start.9 = (s32[16,256]{1,0:T(8,128)S(1)}, s32[16,256]{1,0:T(8,128)}, u32[]{:S(2)}) copy-start(s32[16,256]{1,0:T(8,128)} %param.17) | copy-start | bytes 49156
  58.5 18.7 %all-to-all-start = ((bf16[4,512,256]{2,1,0:T(8,128)(2,1)}), bf16[4,512,256]{2,1,0:T(8,128)(2,1)S(1)}, u32[]{:S(2)}, u32[]{:S(2)}) async-start(bf16[4,512,256]{2,1,0:T(8,128)(2,1)} %get-tuple-element.21), calls=%async_computation | async-start | bytes 2097152 | tf_op jit(solution)/shard_map/all_to_all | solution.py:99
  71.1 35.2 %copy-start.6 = (pred[1536]{0:T(1024)(128)(4,1)}, pred[1536]{0:T(1024)(128)(4,1)S(1)}, u32[]{:S(2)}) copy-start(pred[1536]{0:T(1024)(128)(4,1)S(1)} %get-tuple-element.12) | copy-start | bytes 4612
  77.2 18.8 %all-to-all-start.1 = ((bf16[4,512,256]{2,1,0:T(8,128)(2,1)}), bf16[4,512,256]{2,1,0:T(8,128)(2,1)}, u32[]{:S(2)}, u32[]{:S(2)}) async-start(bf16[4,512,256]{2,1,0:T(8,128)(2,1)} %get-tuple-element.20), calls=%async_computation.1 | async-start | bytes 2097152 | tf_op jit(solution)/shard_map/all_to_all | solution.py:100
  81.4 324.9 %all-reduce.3.cloned.1.call-start = ((), (), s32[]{:S(2)}) async-start(), calls=%async_computation.2 | async-start | bytes 3145728 | tf_op jit(solution)/shard_map/psum | solution.py:53
  81.7 24.6 %copy-start.11 = (f32[16384]{0:T(1024)S(1)}, f32[16384]{0:T(1024)}, u32[]{:S(2)}) copy-start(f32[16384]{0:T(1024)} %param.15) | copy-start | bytes 196612
  87.1 17.5 %copy-start.1 = (bf16[1536,256]{1,0:T(8,128)(2,1)S(1)}, bf16[1536,256]{1,0:T(8,128)(2,1)}, u32[]{:S(2)}) copy-start(bf16[1536,256]{1,0:T(8,128)(2,1)} %gather_fusion.3) | copy-start | bytes 2359300
  104.6 1.8 copy-start.4
  106.4 39.1 %copy-start.3 = (bf16[1536,256]{1,0:T(8,128)(2,1)S(1)}, bf16[1536,256]{1,0:T(8,128)(2,1)}, u32[]{:S(2)}) copy-start(bf16[1536,256]{1,0:T(8,128)(2,1)} %fusion.16.clone.5) | copy-start | bytes 2359300
  253.5 67.2 %copy-start.10 = (f32[1536]{0:T(1024)S(1)}, f32[1536]{0:T(1024)}, u32[]{:S(2)}) copy-start(f32[1536]{0:T(1024)} %get-tuple-element.9) | copy-start | bytes 18436
  253.5 152.8 %copy-start.2 = (bf16[1536,256]{1,0:T(8,128)(2,1)S(1)}, bf16[1536,256]{1,0:T(8,128)(2,1)}, u32[]{:S(2)}) copy-start(bf16[1536,256]{1,0:T(8,128)(2,1)} %gather_fusion.3) | copy-start | bytes 2359300
  253.5 152.8 %copy-start.7 = (pred[1536]{0:T(1024)(128)(4,1)S(1)}, pred[1536]{0:T(1024)(128)(4,1)}, u32[]{:S(2)}) copy-start(pred[1536]{0:T(1024)(128)(4,1)} %copy-done.6) | copy-start | bytes 4612
  253.5 154.7 %copy-start.5 = (f32[1536]{0:T(1024)S(1)}, f32[1536]{0:T(1024)}, u32[]{:S(2)}) copy-start(f32[1536]{0:T(1024)} %copy-done.4) | copy-start | bytes 18436
  253.6 154.7 %copy-start.8 = (f32[1536]{0:T(1024)S(1)}, f32[1536]{0:T(1024)}, u32[]{:S(2)}) copy-start(f32[1536]{0:T(1024)} %get-tuple-element.18) | copy-start | bytes 18436
Sparse Core Ops, SparseCore 0:
  320.9 85.3 all-reduce.2
where the time goes:
time: 420 us; the launch traced here: 419 us
  matrix products  176 us (42%)
  waiting for transfers between devices  94.6 us (23%)
  local copies, waits for them, and re-layouts  56.4 us (13%)
  blocking collectives  38.1 us (9%)
  other arithmetic  30.5 us (7%)
  between operations  14.3 us (3%)
  starting transfers between devices  8.75 us (2%)
    psum x1, waiting for transfers between devices, proto_head(): feature_grad = lax.psum(feature_grad, 'proto')  84.9 us
    dot_general x1, matrix products, proto_head(): jnp.dot(student_unit, student_cols, preferred_element_type=jnp.float32)  70 us
    dot_general x1, matrix products, proto_head(): lax.dot_general(logit_grad, student_cols, (((1,), (1,)), ((), ())), prefe...  67.1 us
    dot_general x1, matrix products, proto_head(): jnp.dot(teacher_unit, teacher_cols, preferred_element_type=jnp.float32)  39.1 us
    psum x1, blocking collectives, proto_head(): lax.psum((jnp.sum(student_exp, axis=1), jnp.sum(teacher_exp, axis=1), jnp...  38.1 us
    gather x3, local copies, waits for them, and re-layouts, local(): jnp.take(local_starts, image_ids)  12.6 us
    gather x2, local copies, waits for them, and re-layouts, local(): patch_ids = jnp.take(order_flat, image_ids * patches + within)  11.8 us
    gather x1, local copies, waits for them, and re-layouts, local(): jnp.take(student_flat, row_ids, axis=0)  10.3 us
  transfers between devices with their start and end apart: 3, of which 3 were waited for; matrix products, arithmetic and copies ran while one was open for 5% of the time, Pallas kernels for 0%

commit v1 on v0

--- a/solution.py
+++ b/solution.py
@@ -7,6 +7,15 @@
 STUDENT_TEMP = 0.1
 TEACHER_TEMP = 0.07
 EPSILON = 1e-06
+
+
+def doubling_sum(array, axis):
+    n_dev = lax.axis_size(axis)
+    total, far = (array, 1)
+    while far < n_dev:
+        total = total + lax.ppermute(total, axis, [(i, i ^ far) for i in range(n_dev)])
+        far = 2 * far
+    return total
 
 
 def norm_columns(weights):
@@ -50,7 +59,7 @@
     feature_grad = lax.dot_general(
         logit_grad, student_cols, (((1,), (1,)), ((), ())), preferred_element_type=jnp.float32
     )
-    feature_grad = lax.psum(feature_grad, "proto")
+    feature_grad = doubling_sum(feature_grad, "proto")
     input_grad = backward(student_in, student_norm, feature_grad)
     return (row_losses, input_grad)
 

time: 420 us -> 435 us (1.036)
  waiting for transfers between devices: 94.6 us -> 125 us
  between operations: 14.3 us -> 0.97 us
  other arithmetic: 30.5 us -> 25.4 us
    ppermute x0 -> x3, waiting for transfers between devices: none -> 117 us  [doubling_sum(): lax.ppermute(total, axis, [(i, i ^ far) for i in range(n_dev)])]
    psum x1 -> x0, waiting for transfers between devices: 84.9 us -> none  [proto_head(): feature_grad = lax.psum(feature_grad, 'proto')]
    all_to_all x1, waiting for transfers between devices: 8.82 us -> 0.83 us  [local(): lax.all_to_all(send_teacher, 'dp', split_axis=0, concat_axis=0, tiled=True)]
    all_to_all x1, waiting for transfers between devices: 0.87 us -> 7.24 us  [local(): lax.all_to_all(send_student, 'dp', split_axis=0, concat_axis=0, tiled=True)]
  transfers between devices with their start and end apart: 3 -> 5, of which waited for: 3 -> 5; matrix products, arithmetic and copies ran while one was open for 5% -> 5% of each run, Pallas kernels for 0% -> 0%
where the time goes in v1:
time: 435 us; the launch traced here: 434 us
  matrix products  176 us (40%)
  waiting for transfers between devices  125 us (29%)
  local copies, waits for them, and re-layouts  59 us (14%)
  blocking collectives  38.1 us (9%)
  other arithmetic  25.4 us (6%)
  starting transfers between devices  8.92 us (2%)
    ppermute x3, waiting for transfers between devices, doubling_sum(): lax.ppermute(total, axis, [(i, i ^ far) for i in range(n_dev)])  117 us
    dot_general x1, matrix products, proto_head(): jnp.dot(student_unit, student_cols, preferred_element_type=jnp.float32)  69.8 us
    dot_general x1, matrix products, proto_head(): lax.dot_general(logit_grad, student_cols, (((1,), (1,)), ((), ())), prefe...  67.5 us
    dot_general x1, matrix products, proto_head(): jnp.dot(teacher_unit, teacher_cols, preferred_element_type=jnp.float32)  39 us
    psum x1, blocking collectives, proto_head(): lax.psum((jnp.sum(student_exp, axis=1), jnp.sum(teacher_exp, axis=1), jnp...  38.1 us
    gather x3, local copies, waits for them, and re-layouts, local(): jnp.take(local_starts, image_ids)  12.6 us
    gather x2, local copies, waits for them, and re-layouts, local(): patch_ids = jnp.take(order_flat, image_ids * patches + within)  11.8 us
    gather x1, local copies, waits for them, and re-layouts, local(): jnp.take(student_flat, row_ids, axis=0)  10.3 us
  transfers between devices with their start and end apart: 5, of which 5 were waited for; matrix products, arithmetic and copies ran while one was open for 5% of the time, Pallas kernels for 0%

profile of v1, /device:TPU:0, one launch (start us, length us, event | category | flops | bytes accessed | tf_op | source)
XLA Modules:
  0.0 433.9 jit_solution(728283697706798864)
XLA Ops:
  0.6 0.0 copy-start
  0.6 0.0 copy-start.8
  0.7 0.9 reshape.344
  1.6 0.7 dynamic-slice_bitcast_fusion
  2.3 0.1 copy.15
  2.4 0.1 reduce.1
  2.5 0.7 dynamic-slice_subtract_fusion
  3.3 0.1 reduce_sum.119
  3.4 0.2 reduce-window.16
  3.6 0.6 fusion.33
  4.2 0.7 and_select_fusion
  4.9 0.1 broadcast_add_fusion
  4.9 0.1 convert_reduce_fusion
  5.1 12.6 %gather_fusion = s32[2048]{0:T(1024)S(1)} fusion(s32[16]{0:T(128)S(1)} %dynamic-slice_subtract_fusion, s32[2048]{0:T(1024)S(1)} %broadcast_clamp_fusion.2), kind=kCustom, calls=%fused_computation.4 | custom fusion | bytes 24576 | tf_op jit(solution)/shard_map/jit(_take)/gather | solution.py:101
  17.7 0.0 copy-done.8
  17.7 0.1 fusion.27
  17.8 11.8 %gather_fusion.1 = s32[2048]{0:T(1024)S(1)} fusion(s32[4096]{0:T(1024)S(1)} %bitcast.42, s32[2048]{0:T(1024)S(1)} %broadcast_clamp_fusion.1), kind=kCustom, calls=%fused_computation.5 | custom fusion | bytes 24576 | tf_op jit(solution)/shard_map/jit(_take)/gather | solution.py:102
  29.6 0.7 compare_and_fusion.1
  30.4 0.0 copy-done
  30.4 7.5 %gather_fusion.4 = bf16[2048,256]{1,0:T(8,128)(2,1)S(1)} fusion(bf16[4096,256]{1,0:T(8,128)(2,1)S(1)} %bitcast.41, s32[2048]{0:T(1024)S(1)} %broadcast_clamp_fusion), kind=kCustom, calls=%fused_computation.2.clone | custom fusion | bytes 2105344 | tf_op jit(solution)/shard_map/jit(_take)/gather | solution.py:106
  37.9 10.3 %gather_fusion.2 = bf16[2048,256]{1,0:T(8,128)(2,1)} fusion(bf16[4096,256]{1,0:T(8,128)(2,1)} %bitcast.44, s32[2048]{0:T(1024)S(1)} %broadcast_clamp_fusion), kind=kCustom, calls=%fused_computation.clone | custom fusion | bytes 2105344 | tf_op jit(solution)/shard_map/jit(_take)/gather | solution.py:105
  48.2 3.7 select_select_fusion
  51.9 4.3 all-to-all-start.1
  56.2 5.1 %fusion.3 = f32[16384]{0:T(1024)S(1)} fusion(bf16[256,16384]{1,0:T(8,128)(2,1)} %param.14), kind=kLoop, calls=%fused_computation.17 | loop fusion | flops 12566528 | bytes 8454144 | tf_op jit(solution)/shard_map/reduce_sum | solution.py:23
  61.3 0.6 fusion.41
  62.0 0.1 convert_reduce_fusion.1
  62.1 2.5 fusion.32
  64.7 0.0 copy-start.5
  64.7 5.1 %fusion.1 = f32[16384]{0:T(1024)S(1)} fusion(bf16[256,16384]{1,0:T(8,128)(2,1)} %param.13), kind=kLoop, calls=%fused_computation.15 | loop fusion | flops 12566528 | bytes 8454144 | tf_op jit(solution)/shard_map/reduce_sum | solution.py:23
  69.8 0.8 all-to-all-done.1
  70.6 4.4 %all-to-all-start = ((bf16[4,512,256]{2,1,0:T(8,128)(2,1)}), bf16[4,512,256]{2,1,0:T(8,128)(2,1)}, u32[]{:S(2)}, u32[]{:S(2)}) async-start(bf16[4,512,256]{2,1,0:T(8,128)(2,1)} %get-tuple-element.25), calls=%async_computation | async-start | bytes 2097152 | tf_op jit(solution)/shard_map/all_to_all | solution.py:108
  75.1 0.0 copy-start.10
  75.1 5.4 %gather_fusion.5 = bf16[1536,256]{1,0:T(8,128)(2,1)} fusion(bf16[2048,256]{1,0:T(8,128)(2,1)S(1)} %bitcast.43, s32[2048]{0:T(1024)S(1)} %pad_clamp_fusion), kind=kCustom, calls=%fused_computation.3.clone | custom fusion | bytes 1579008 | tf_op jit(solution)/shard_map/jit(_take)/gather | solution.py:114
  80.5 1.6 fusion.7
  82.1 7.2 %all-to-all-done = bf16[4,512,256]{2,1,0:T(8,128)(2,1)} async-done(((bf16[4,512,256]{2,1,0:T(8,128)(2,1)}), bf16[4,512,256]{2,1,0:T(8,128)(2,1)}, u32[]{:S(2)}, u32[]{:S(2)}) %all-to-all-start) | async-done | bytes 1048608 | tf_op jit(solution)/shard_map/all_to_all | solution.py:108
  89.4 5.8 %gather_fusion.3 = bf16[1536,256]{1,0:T(8,128)(2,1)} fusion(bf16[2048,256]{1,0:T(8,128)(2,1)} %bitcast.10, s32[2048]{0:T(1024)S(1)} %pad_clamp_fusion), kind=kCustom, calls=%fused_computation.1.clone | custom fusion | bytes 1579008 | tf_op jit(solution)/shard_map/jit(_take)/gather | solution.py:111
  95.2 1.4 copy.16
  96.6 0.0 copy-start.1
  96.7 0.2 fusion.9
  96.9 0.7 multiply_multiply_fusion
  97.5 0.0 copy-done.10
  97.5 39.0 %multiply_exponential_fusion = f32[1536,16384]{1,0:T(8,128)} fusion(f32[16384]{0:T(1024)S(1)} %copy-done.10, bf16[256,16384]{1,0:T(8,128)(2,1)} %param.14, f32[16384]{0:T(1024)S(1)} %add_sqrt_fusion, f32[1536]{0:T(1024)S(1)} %add_sqrt_fusion.2, bf16[1536,256]{1,0:T(8,128)(2,1)} %gather_fusion.5, pred[1536]{0:T(1024)(128)(4,1)S(1)} %get-tuple-element.16), kind=kOutput, calls=%fused_computation.8 | convolution fusion | flops 12949389312 | bytes 109977088 | tf_op jit(solution)/shard_map/dot_general | solution.py:43
  136.5 0.0 copy-done.5
  136.5 0.0 copy-done.1
  136.5 0.0 copy-done.3
  136.5 69.8 %exponential_reduce_fusion = (f32[1536]{0:T(1024)S(1)}, f32[1536]{0:T(1024)S(1)}, f32[1536]{0:T(1024)S(1)}, f32[1536,16384]{1,0:T(8,128)}) fusion(f32[1536,16384]{1,0:T(8,128)} %multiply_exponential_fusion, bf16[256,16384]{1,0:T(8,128)(2,1)} %param.13, f32[16384]{0:T(1024)S(1)} %add_sqrt_fusion.1, f32[1536]{0:T(1024)S(1)} %get-tuple-element.23, ...), kind=kOutput, calls=%fused_computation.9 | convolution fusion | flops 13024880640 | bytes 210593280 | tf_op jit(solution)/shard_map/dot_general | solution.py:42
  206.3 38.1 %all-reduce = (f32[1536]{0:T(1024)}, f32[1536]{0:T(1024)S(1)}, f32[1536]{0:T(1024)S(1)}) all-reduce(f32[1536]{0:T(1024)S(1)} %get-tuple-element.11, f32[1536]{0:T(1024)S(1)} %get-tuple-element.12, f32[1536]{0:T(1024)S(1)} %get-tuple-element.10), channel_id=1, replica_groups=mesh['dp'=4,'proto'=8] {'proto'}, use_global_device_ids=true, to_apply=%region_14.17 | all-reduce | flops 4608 | bytes 36864 | tf_op jit(solution)/shard_map/psum | solution.py:46
  244.4 67.5 %fusion = f32[1536,256]{0,1:T(8,128)} fusion(f32[1536,16384]{1,0:T(8,128)} %multiply_exponential_fusion, f32[1536,16384]{1,0:T(8,128)} %get-tuple-element.32, f32[1536]{0:T(1024)S(1)} %get-tuple-element.14, f32[1536]{0:T(1024)S(1)} %get-tuple-element.15, bf16[256,16384]{1,0:T(8,128)(2,1)} %param.13, f32[16384]{0:T(1024)S(1)} %add_sqrt_fusion.1), kind=kOutput, calls=%fused_computation.10 | convolution fusion | flops 13048479744 | bytes 211365888 | tf_op jit(solution)/shard_map/dot_general | solution.py:59
  311.9 0.0 copy-start.4
  311.9 0.1 collective-permute-start
  312.0 28.8 %collective-permute-done = f32[1536,256]{0,1:T(8,128)S(1)} collective-permute-done((f32[1536,256]{0,1:T(8,128)}, f32[1536,256]{0,1:T(8,128)S(1)}, u32[]{:S(2)}, u32[]{:S(2)}) %collective-permute-start) | collective-permute-done | bytes 1572896 | tf_op jit(solution)/shard_map/ppermute | solution.py:16
  340.8 1.7 add.245
  342.4 0.1 collective-permute-start.1
  342.5 32.1 %collective-permute-done.1 = f32[1536,256]{0,1:T(8,128)S(1)} collective-permute-done((f32[1536,256]{0,1:T(8,128)S(1)}, f32[1536,256]{0,1:T(8,128)S(1)}, u32[]{:S(2)}, u32[]{:S(2)}) %collective-permute-start.1) | collective-permute-done | bytes 1572896 | tf_op jit(solution)/shard_map/ppermute | solution.py:16
  374.6 0.2 add.246
  374.8 0.1 collective-permute-start.2
  374.9 0.6 broadcast_in_dim.84
  375.5 56.4 %collective-permute-done.2 = f32[1536,256]{0,1:T(8,128)S(1)} collective-permute-done((f32[1536,256]{0,1:T(8,128)S(1)}, f32[1536,256]{0,1:T(8,128)S(1)}, u32[]{:S(2)}, u32[]{:S(2)}) %collective-permute-start.2) | collective-permute-done | bytes 1572896 | tf_op jit(solution)/shard_map/ppermute | solution.py:16
  431.9 0.0 copy-done.6
  431.9 0.4 fusion.11
  432.3 0.0 copy-done.4
  432.3 0.0 copy-done.7
  432.3 0.5 fusion.20
  432.8 1.2 copy.17
  (27 shorter events, 0.2 us)
Async XLA Ops:
  0.6 29.8 %copy-start = (bf16[16,256,256]{2,1,0:T(8,128)(2,1)S(1)}, bf16[16,256,256]{2,1,0:T(8,128)(2,1)}, u32[]{:S(2)}) copy-start(bf16[16,256,256]{2,1,0:T(8,128)(2,1)} %param.12) | copy-start | bytes 6291460
  0.6 17.1 %copy-start.8 = (s32[16,256]{1,0:T(8,128)S(1)}, s32[16,256]{1,0:T(8,128)}, u32[]{:S(2)}) copy-start(s32[16,256]{1,0:T(8,128)} %param.17) | copy-start | bytes 49156
  51.9 18.7 %all-to-all-start.1 = ((bf16[4,512,256]{2,1,0:T(8,128)(2,1)}), bf16[4,512,256]{2,1,0:T(8,128)(2,1)S(1)}, u32[]{:S(2)}, u32[]{:S(2)}) async-start(bf16[4,512,256]{2,1,0:T(8,128)(2,1)} %get-tuple-element.24), calls=%async_computation.1 | async-start | bytes 2097152 | tf_op jit(solution)/shard_map/all_to_all | solution.py:109
  64.7 71.9 %copy-start.5 = (pred[1536]{0:T(1024)(128)(4,1)}, pred[1536]{0:T(1024)(128)(4,1)S(1)}, u32[]{:S(2)}) copy-start(pred[1536]{0:T(1024)(128)(4,1)S(1)} %get-tuple-element.16) | copy-start | bytes 4612
  70.6 18.8 %all-to-all-start = ((bf16[4,512,256]{2,1,0:T(8,128)(2,1)}), bf16[4,512,256]{2,1,0:T(8,128)(2,1)}, u32[]{:S(2)}, u32[]{:S(2)}) async-start(bf16[4,512,256]{2,1,0:T(8,128)(2,1)} %get-tuple-element.25), calls=%async_computation | async-start | bytes 2097152 | tf_op jit(solution)/shard_map/all_to_all | solution.py:108
  75.1 22.4 %copy-start.10 = (f32[16384]{0:T(1024)S(1)}, f32[16384]{0:T(1024)}, u32[]{:S(2)}) copy-start(f32[16384]{0:T(1024)} %param.15) | copy-start | bytes 196612
  96.6 39.9 %copy-start.1 = (bf16[1536,256]{0,1:T(8,128)(2,1)}, bf16[1536,256]{0,1:T(8,128)(2,1)S(1)}, u32[]{:S(2)}) copy-start(bf16[1536,256]{0,1:T(8,128)(2,1)S(1)} %copy.16) | copy-start | bytes 2359300
  97.5 39.0 %copy-start.3 = (f32[1536]{0:T(1024)}, f32[1536]{0:T(1024)S(1)}, u32[]{:S(2)}) copy-start(f32[1536]{0:T(1024)S(1)} %get-tuple-element.23) | copy-start | bytes 18436
  311.9 63.0 %copy-start.9 = (f32[1536]{0:T(1024)S(1)}, f32[1536]{0:T(1024)}, u32[]{:S(2)}) copy-start(f32[1536]{0:T(1024)} %get-tuple-element.13) | copy-start | bytes 18436
  311.9 120.0 %copy-start.2 = (bf16[1536,256]{0,1:T(8,128)(2,1)S(1)}, bf16[1536,256]{0,1:T(8,128)(2,1)}, u32[]{:S(2)}) copy-start(bf16[1536,256]{0,1:T(8,128)(2,1)} %copy-done.1) | copy-start | bytes 2359300
  311.9 120.0 %copy-start.6 = (pred[1536]{0:T(1024)(128)(4,1)S(1)}, pred[1536]{0:T(1024)(128)(4,1)}, u32[]{:S(2)}) copy-start(pred[1536]{0:T(1024)(128)(4,1)} %copy-done.5) | copy-start | bytes 4612
  311.9 120.4 %copy-start.4 = (f32[1536]{0:T(1024)S(1)}, f32[1536]{0:T(1024)}, u32[]{:S(2)}) copy-start(f32[1536]{0:T(1024)} %copy-done.3) | copy-start | bytes 18436
  311.9 120.4 %copy-start.7 = (f32[1536]{0:T(1024)S(1)}, f32[1536]{0:T(1024)}, u32[]{:S(2)}) copy-start(f32[1536]{0:T(1024)} %get-tuple-element.22) | copy-start | bytes 18436
  311.9 28.8 %collective-permute-start = (f32[1536,256]{0,1:T(8,128)}, f32[1536,256]{0,1:T(8,128)S(1)}, u32[]{:S(2)}, u32[]{:S(2)}) collective-permute-start(f32[1536,256]{0,1:T(8,128)} %fusion), channel_id=1, source_target_pairs={{0,1},{1,0},{2,3},{3,2},{4,5},{5,4},{6,7},{7,6},{8,9},{9,8},{10,11... | collective-permute-start | bytes 4718600 | tf_op jit(solution)/shard_map/ppermute | solution.py:16
  342.4 32.2 %collective-permute-start.1 = (f32[1536,256]{0,1:T(8,128)S(1)}, f32[1536,256]{0,1:T(8,128)S(1)}, u32[]{:S(2)}, u32[]{:S(2)}) collective-permute-start(f32[1536,256]{0,1:T(8,128)S(1)} %add.245), channel_id=1, source_target_pairs={{0,2},{1,3},{2,0},{3,1},{4,6},{5,7},{6,4},{7,5},{8,10},{9,11},{10,... | collective-permute-start | bytes 4718600 | tf_op jit(solution)/shard_map/ppermute | solution.py:16
  374.8 57.1 %collective-permute-start.2 = (f32[1536,256]{0,1:T(8,128)S(1)}, f32[1536,256]{0,1:T(8,128)S(1)}, u32[]{:S(2)}, u32[]{:S(2)}) collective-permute-start(f32[1536,256]{0,1:T(8,128)S(1)} %add.246), channel_id=1, source_target_pairs={{0,4},{1,5},{2,6},{3,7},{4,0},{5,1},{6,2},{7,3},{8,12},{9,13},{10,... | collective-permute-start | bytes 4718600 | tf_op jit(solution)/shard_map/ppermute | solution.py:16
